TPU v7x, 32 devices: a whole 2x2x4 slice. The times are simulated.
32 devices in a mesh: mz: 4 (over z), px: 8 (over y, x, core).
Axes of the slice: x: 2, y: 2, z: 4, core: 2. Of those that a mesh axis runs over, the one named last changes fastest.
Arguments:
- spectra: float32 [3072, 12288], P('px', 'mz'), may hold values from 0 to 10
- w_factor: float32 [48, 3072], P(None, ('px', 'mz')), may hold values from 0.05 to 1
- h_factor: float32 [48, 12288], P(None, ('mz', 'px')), may hold values from 0.05 to 1
Outputs:
- w_final: float32 [48, 3072], P(None, ('px', 'mz'))
- h_final: float32 [48, 12288], P(None, ('mz', 'px'))
- misfit: float32 [3072], P(('px', 'mz'))
All inputs are finite; a program needn't handle non-finite values.
Results may differ from a plain program's by a relative error of at most 0.0001.
Values sent between devices are 32-bit elements; how exact they have to be, the bound alone decides.
No kernel may reach another device: no remote copies, remote signals or barrier semaphores. Data moves between devices by JAX's collectives and lax.ppermute only.
A program may use at most 64 MiB of HBM per device.

v0:
```python
import jax
import jax.numpy as jnp
from jax import lax
from jax.sharding import PartitionSpec as P

ITERS = 3


def matmul(left, right):
    return jnp.dot(left, right, preferred_element_type=jnp.float32, precision=lax.Precision.HIGHEST)


def rows_of(w_piece):
    return lax.all_gather(w_piece, "mz", axis=1, tiled=True)


def loading_gram(w_block):
    return lax.psum(matmul(w_block, w_block.T), "px")


def spectral_gram(h_block):
    return lax.psum(matmul(h_block, h_block.T), "mz")


def per_device(spectra, w_factor, h_factor):
    w_piece = w_factor
    h_piece = h_factor
    w_block = rows_of(w_piece)
    h_block = h_piece
    for iteration in range(ITERS):
        numerator = lax.psum_scatter(
            matmul(w_block, spectra), "px", scatter_dimension=1, tiled=True
        )
        gram_w = loading_gram(w_block)
        h_piece = h_piece * numerator / matmul(gram_w, h_piece)
        h_block = lax.all_gather(h_piece, "px", axis=1, tiled=True)
        numerator = lax.psum_scatter(
            matmul(h_block, spectra.T), "mz", scatter_dimension=1, tiled=True
        )
        gram_h = spectral_gram(h_block)
        w_piece = w_piece * numerator / matmul(gram_h, w_piece)
        w_block = rows_of(w_piece)
    difference = spectra - matmul(w_block.T, h_block)
    partial_error = jnp.sum(difference * difference, axis=1)
    misfit = lax.psum_scatter(partial_error, "mz", scatter_dimension=0, tiled=True)
    return (w_piece, h_piece, misfit)


def solution(mesh):
    in_specs = (P("px", "mz"), P(None, ("px", "mz")), P(None, ("mz", "px")))
    out_specs = (P(None, ("px", "mz")), P(None, ("mz", "px")), P(("px", "mz")))
    return jax.shard_map(
        per_device, mesh=mesh, in_specs=in_specs, out_specs=out_specs, check_vma=False
    )
```

profile of v0, /device:TPU:0, one launch (start us, length us, event | category | flops | bytes accessed | tf_op | source)
XLA Modules:
  0.0 318.1 jit_solution(4339543671412896273)
XLA Ops:
  7.2 15.3 %all-gather = f32[4,96,48]{1,2,0:T(8,128)S(1)} all-gather(f32[1,96,48]{1,2,0:T(8,128)} %bitcast.70), channel_id=1, replica_groups=mesh['mz'=4,'px'=8] {'mz'}, dimensions={0}, use_global_device_ids=true | all-gather | bytes 92160 | tf_op jit(solution)/shard_map/all_gather | solution.py:14
  22.5 0.1 reshape.7
  22.7 6.1 %fusion = f32[48,3072]{1,0:T(8,128)} fusion(f32[384,48]{0,1:T(8,128)S(1)} %reshape.7, f32[384,3072]{1,0:T(8,128)} %param.3), kind=kOutput, calls=%fused_computation.10 | convolution fusion | flops 679477248 | bytes 5382144 | tf_op jit(solution)/shard_map/dot_general | solution.py:10
  28.8 0.2 fusion.1
  29.0 22.5 %psum.42 = f32[48,48]{1,0:T(8,128)S(1)} all-reduce(f32[48,48]{1,0:T(8,128)S(1)} %fusion.1), channel_id=1, replica_groups=mesh['mz'=4,'px'=8] {'px'}, use_global_device_ids=true, to_apply=%region_1.0 | all-reduce | flops 2304 | bytes 18432 | tf_op jit(solution)/shard_map/psum | solution.py:18
  51.5 11.9 %reduce-scatter.13.cloned.1.call-done = f32[48,384]{1,0:T(8,128)} async-done(((f32[48,3072]{1,0:T(8,128)}), f32[48,384]{1,0:T(8,128)}) %reduce-scatter.13.cloned.1.call-update) | async-done | bytes 73744 | tf_op jit(solution)/shard_map/reduce_scatter | solution.py:31
  63.4 1.1 convolution_divide_fusion.2
  64.5 10.4 %all_gather.22 = f32[48,3072]{1,0:T(8,128)S(1)} all-gather(f32[48,384]{1,0:T(8,128)S(1)} %convolution_divide_fusion.2), channel_id=1, replica_groups=mesh['mz'=4,'px'=8] {'px'}, dimensions={1}, use_global_device_ids=true | all-gather | bytes 663552 | tf_op jit(solution)/shard_map/all_gather | solution.py:36
  74.8 6.3 %convolution_bitcast_fusion.2 = f32[384,48]{1,0:T(8,128)} fusion(f32[48,3072]{1,0:T(8,128)S(1)} %all_gather.22, f32[384,3072]{1,0:T(8,128)} %param.3), kind=kOutput, calls=%fused_computation.3 | convolution fusion | flops 679477248 | bytes 5382144
  81.2 0.6 fusion.2
  81.8 19.1 %psum.43 = f32[48,48]{1,0:T(8,128)S(1)} all-reduce(f32[48,48]{1,0:T(8,128)S(1)} %fusion.2), channel_id=1, replica_groups=mesh['mz'=4,'px'=8] {'mz'}, use_global_device_ids=true, to_apply=%region_3.0 | all-reduce | flops 2304 | bytes 18432 | tf_op jit(solution)/shard_map/psum | solution.py:22
  100.9 0.1 reduce-scatter.19.cloned.1.call-done
  101.0 0.9 copy.15
  101.9 0.2 convolution_divide_fusion.5
  102.1 13.3 %all-gather.1 = f32[4,96,48]{1,2,0:T(8,128)S(1)} all-gather(f32[1,96,48]{1,2,0:T(8,128)S(1)} %bitcast.69), channel_id=1, replica_groups=mesh['mz'=4,'px'=8] {'mz'}, dimensions={0}, use_global_device_ids=true | all-gather | bytes 92160 | tf_op jit(solution)/shard_map/all_gather | solution.py:14
  115.4 0.1 reshape.9
  115.6 6.1 %fusion.3 = f32[48,3072]{1,0:T(8,128)} fusion(f32[384,48]{0,1:T(8,128)S(1)} %reshape.9, f32[384,3072]{1,0:T(8,128)} %param.3), kind=kOutput, calls=%fused_computation.13 | convolution fusion | flops 679477248 | bytes 5382144 | tf_op jit(solution)/shard_map/dot_general | solution.py:10
  121.7 0.0 reduce-scatter.21.cloned.1.call-start
  121.7 0.2 fusion.4
  121.9 22.5 %psum.44 = f32[48,48]{1,0:T(8,128)S(1)} all-reduce(f32[48,48]{1,0:T(8,128)S(1)} %fusion.4), channel_id=1, replica_groups=mesh['mz'=4,'px'=8] {'px'}, use_global_device_ids=true, to_apply=%region_5.0 | all-reduce | flops 2304 | bytes 18432 | tf_op jit(solution)/shard_map/psum | solution.py:18
  144.4 8.9 %reduce-scatter.15.cloned.1.call-done = f32[48,384]{1,0:T(8,128)} async-done(((f32[48,3072]{1,0:T(8,128)}), f32[48,384]{1,0:T(8,128)}) %reduce-scatter.15.cloned.1.call-update) | async-done | bytes 73744 | tf_op jit(solution)/shard_map/reduce_scatter | solution.py:31
  153.3 1.1 convolution_divide_fusion.1
  154.4 10.5 %all_gather.24 = f32[48,3072]{1,0:T(8,128)S(1)} all-gather(f32[48,384]{1,0:T(8,128)S(1)} %convolution_divide_fusion.1), channel_id=1, replica_groups=mesh['mz'=4,'px'=8] {'px'}, dimensions={1}, use_global_device_ids=true | all-gather | bytes 663552 | tf_op jit(solution)/shard_map/all_gather | solution.py:36
  165.0 6.3 %convolution_bitcast_fusion.1 = f32[384,48]{1,0:T(8,128)} fusion(f32[48,3072]{1,0:T(8,128)S(1)} %all_gather.24, f32[384,3072]{1,0:T(8,128)} %param.3), kind=kOutput, calls=%fused_computation.2 | convolution fusion | flops 679477248 | bytes 5382144
  171.3 0.6 fusion.5
  172.0 19.1 %psum.45 = f32[48,48]{1,0:T(8,128)S(1)} all-reduce(f32[48,48]{1,0:T(8,128)S(1)} %fusion.5), channel_id=1, replica_groups=mesh['mz'=4,'px'=8] {'mz'}, use_global_device_ids=true, to_apply=%region_7.0 | all-reduce | flops 2304 | bytes 18432 | tf_op jit(solution)/shard_map/psum | solution.py:22
  191.0 0.1 reduce-scatter.21.cloned.1.call-done
  191.2 0.9 copy.17
  192.0 0.2 convolution_divide_fusion.4
  192.2 13.3 %all-gather.2 = f32[4,96,48]{1,2,0:T(8,128)S(1)} all-gather(f32[1,96,48]{1,2,0:T(8,128)S(1)} %bitcast.68), channel_id=1, replica_groups=mesh['mz'=4,'px'=8] {'mz'}, dimensions={0}, use_global_device_ids=true | all-gather | bytes 92160 | tf_op jit(solution)/shard_map/all_gather | solution.py:14
  205.6 0.1 reshape.11
  205.7 6.1 %fusion.6 = f32[48,3072]{1,0:T(8,128)} fusion(f32[384,48]{0,1:T(8,128)S(1)} %reshape.11, f32[384,3072]{1,0:T(8,128)} %param.3), kind=kOutput, calls=%fused_computation.16 | convolution fusion | flops 679477248 | bytes 5382144 | tf_op jit(solution)/shard_map/dot_general | solution.py:10
  211.9 0.6 dynamic-slice
  213.1 0.2 fusion.7
  213.3 22.4 %psum.46 = f32[48,48]{1,0:T(8,128)S(1)} all-reduce(f32[48,48]{1,0:T(8,128)S(1)} %fusion.7), channel_id=1, replica_groups=mesh['mz'=4,'px'=8] {'px'}, use_global_device_ids=true, to_apply=%region_9.0 | all-reduce | flops 2304 | bytes 18432 | tf_op jit(solution)/shard_map/psum | solution.py:18
  235.7 7.9 %reduce-scatter.17.cloned.1.call-done = f32[48,384]{1,0:T(8,128)} async-done(((f32[48,3072]{1,0:T(8,128)}), f32[48,384]{1,0:T(8,128)}) %reduce-scatter.17.cloned.1.call-update) | async-done | bytes 73744 | tf_op jit(solution)/shard_map/reduce_scatter | solution.py:31
  243.5 1.1 convolution_divide_fusion
  244.7 10.4 %all_gather.26 = f32[48,3072]{1,0:T(8,128)S(1)} all-gather(f32[48,384]{1,0:T(8,128)S(1)} %convolution_divide_fusion), channel_id=1, replica_groups=mesh['mz'=4,'px'=8] {'px'}, dimensions={1}, use_global_device_ids=true | all-gather | bytes 663552 | tf_op jit(solution)/shard_map/all_gather | solution.py:36
  255.0 6.3 %convolution_bitcast_fusion = f32[384,48]{1,0:T(8,128)} fusion(f32[48,3072]{1,0:T(8,128)S(1)} %all_gather.26, f32[384,3072]{1,0:T(8,128)} %param.3), kind=kOutput, calls=%fused_computation.1 | convolution fusion | flops 679477248 | bytes 5382144
  261.3 0.6 fusion.8
  261.9 19.1 %psum.47 = f32[48,48]{1,0:T(8,128)S(1)} all-reduce(f32[48,48]{1,0:T(8,128)S(1)} %fusion.8), channel_id=1, replica_groups=mesh['mz'=4,'px'=8] {'mz'}, use_global_device_ids=true, to_apply=%region_11.0 | all-reduce | flops 2304 | bytes 18432 | tf_op jit(solution)/shard_map/psum | solution.py:22
  281.1 0.9 copy.19
  282.0 0.2 convolution_divide_fusion.3
  282.1 13.3 %all-gather.3 = f32[4,96,48]{1,2,0:T(8,128)S(1)} all-gather(f32[1,96,48]{1,2,0:T(8,128)S(1)} %bitcast.71), channel_id=1, replica_groups=mesh['mz'=4,'px'=8] {'mz'}, dimensions={0}, use_global_device_ids=true | all-gather | bytes 92160 | tf_op jit(solution)/shard_map/all_gather | solution.py:14
  295.5 0.1 reshape.13
  295.6 6.0 %multiply_reduce_fusion = f32[384]{0:T(512)S(1)} fusion(f32[384,3072]{1,0:T(8,128)} %param.3, f32[384,48]{0,1:T(8,128)S(1)} %reshape.13, f32[48,3072]{1,0:T(8,128)S(1)} %all_gather.26), kind=kOutput, calls=%fused_computation | convolution fusion | flops 683015808 | bytes 5383680 | tf_op jit(solution)/shard_map/dot_general | solution.py:10
  301.7 8.9 %all-reduce = f32[384]{0:T(512)S(1)} all-reduce(f32[384]{0:T(512)S(1)} %multiply_reduce_fusion), channel_id=8, replica_groups=mesh['mz'=4,'px'=8] {'mz'}, use_global_device_ids=true, to_apply=%region_13.0.clone | all-reduce | flops 384 | bytes 3072
  310.6 0.6 dynamic-slice.1
  (26 shorter events, 0.5 us)
Async XLA Ops:
  7.2 56.2 %copy-start.3 = (f32[48,384]{1,0:T(8,128)S(1)}, f32[48,384]{1,0:T(8,128)}, u32[]{:S(2)}) copy-start(f32[48,384]{1,0:T(8,128)} %param.5) | copy-start | bytes 221188
  7.2 56.2 %reduce-scatter.13.cloned.1.call-start = ((), (), s32[]{:S(2)}) async-start(), calls=%async_computation.6 | async-start | bytes 663552 | tf_op jit(solution)/shard_map/reduce_scatter | solution.py:31
  28.7 73.1 %copy-start = (f32[48,96]{1,0:T(8,128)S(1)}, f32[48,96]{1,0:T(8,128)}, u32[]{:S(2)}) copy-start(f32[48,96]{1,0:T(8,128)} %param.4) | copy-start | bytes 55300
  28.8 72.3 %reduce-scatter.19.cloned.1.call-start = ((), (), s32[]{:S(2)}) async-start(), calls=%async_computation.9 | async-start | bytes 245760
  81.1 72.2 %reduce-scatter.15.cloned.1.call-start = ((), (), s32[]{:S(2)}) async-start(), calls=%async_computation.7 | async-start | bytes 663552 | tf_op jit(solution)/shard_map/reduce_scatter | solution.py:31
  121.7 69.5 %reduce-scatter.21.cloned.1.call-start = ((), (), s32[]{:S(2)}) async-start(), calls=%async_computation.10 | async-start | bytes 245760
  171.3 40.6 %copy-start.4 = (u32[32]{0:T(128)S(1)}, u32[32]{0:T(128)}, u32[]{:S(2)}) copy-start(u32[32]{0:T(128)} %constant.4) | copy-start | bytes 388
  171.3 72.2 %reduce-scatter.17.cloned.1.call-start = ((), (), s32[]{:S(2)}) async-start(), calls=%async_computation.8 | async-start | bytes 663552 | tf_op jit(solution)/shard_map/reduce_scatter | solution.py:31
  211.8 69.3 %reduce-scatter.23.cloned.1.call-start = ((), (), s32[]{:S(2)}) async-start(), calls=%async_computation.11 | async-start | bytes 245760
  244.6 57.0 %copy-start.2 = (f32[48,384]{1,0:T(8,128)}, f32[48,384]{1,0:T(8,128)S(1)}, u32[]{:S(2)}) copy-start(f32[48,384]{1,0:T(8,128)S(1)} %convolution_divide_fusion) | copy-start | bytes 221188
  282.1 29.1 %copy-start.1 = (f32[48,96]{1,0:T(8,128)}, f32[48,96]{1,0:T(8,128)S(1)}, u32[]{:S(2)}) copy-start(f32[48,96]{1,0:T(8,128)S(1)} %convolution_divide_fusion.3) | copy-start | bytes 55300
Sparse Core Ops, SparseCore 0:
  28.9 34.4 reduce-scatter.12
  81.3 19.6 reduce-scatter.18
  121.8 31.5 reduce-scatter.14
  171.4 19.6 reduce-scatter.20
  211.9 31.5 reduce-scatter.16
  261.4 19.5 reduce-scatter.22
where the time goes:
time: 319 us; the launch traced here: 318 us
  blocking collectives  220 us (69%)
  matrix products  49.4 us (15%)
  waiting for transfers between devices  29 us (9%)
  between operations  15 us (5%)
  local copies, waits for them, and re-layouts  4.36 us (1%)
    psum x3, blocking collectives, loading_gram(): return lax.psum(matmul(w_block, w_block.T), 'px')  67.3 us
    psum x3, blocking collectives, spectral_gram(): return lax.psum(matmul(h_block, h_block.T), 'mz')  57.3 us
    all_gather x4, blocking collectives, rows_of(): return lax.all_gather(w_piece, 'mz', axis=1, tiled=True)  55.3 us
    all_gather x3, blocking collectives, per_device(): h_block = lax.all_gather(h_piece, 'px', axis=1, tiled=True)  31.2 us
    dot_general x16, matrix products, matmul(): jnp.dot(left, right, preferred_element_type=jnp.float32, precision=lax.Pr...  30.5 us
    reduce_scatter x3, waiting for transfers between devices, per_device(): lax.psum_scatter(matmul(w_block, spectra), 'px', scatter_dimension=1, til...  28.7 us
    unnamed x3, matrix products  18.9 us
    unnamed x1, blocking collectives  8.95 us
  transfers between devices with their start and end apart: 6, of which 5 were waited for; matrix products, arithmetic and copies ran while one was open for 1% of the time, Pallas kernels for 0%

commit v1 on v0

--- a/solution.py
+++ b/solution.py
@@ -33,7 +33,9 @@
         )
         gram_w = loading_gram(w_block)
         h_piece = h_piece * numerator / matmul(gram_w, h_piece)
-        h_block = lax.all_gather(h_piece, "px", axis=1, tiled=True)
+        h_block = jnp.concatenate(
+            lax.all_to_all(jnp.stack([h_piece] * lax.axis_size("px")), "px", 0, 0), axis=1
+        )
         numerator = lax.psum_scatter(
             matmul(h_block, spectra.T), "mz", scatter_dimension=1, tiled=True
         )

time: 319 us -> 326 us (1.022)
  blocking collectives: 220 us -> 227 us
    all_to_all x0 -> x3, blocking collectives: none -> 38.8 us  [per_device(): lax.all_to_all(jnp.stack([h_piece] * lax.axis_size('px')), 'px', 0, 0)]
    all_gather x3 -> x0, blocking collectives: 31.2 us -> none  [per_device(): h_block = lax.all_gather(h_piece, 'px', axis=1, tiled=True)]
  transfers between devices with their start and end apart: 6 -> 6, of which waited for: 5 -> 3; matrix products, arithmetic and copies ran while one was open for 1% -> 1% of each run, Pallas kernels for 0% -> 0%
where the time goes in v1:
time: 326 us; the launch traced here: 325 us
  blocking collectives  227 us (70%)
  matrix products  49.4 us (15%)
  waiting for transfers between devices  28.5 us (9%)
  between operations  15 us (5%)
  local copies, waits for them, and re-layouts  4.61 us (1%)
    psum x3, blocking collectives, loading_gram(): return lax.psum(matmul(w_block, w_block.T), 'px')  67.3 us
    psum x3, blocking collectives, spectral_gram(): return lax.psum(matmul(h_block, h_block.T), 'mz')  57.3 us
    all_gather x4, blocking collectives, rows_of(): return lax.all_gather(w_piece, 'mz', axis=1, tiled=True)  55.1 us
    all_to_all x3, blocking collectives, per_device(): lax.all_to_all(jnp.stack([h_piece] * lax.axis_size('px')), 'px', 0, 0)  38.8 us
    dot_general x16, matrix products, matmul(): jnp.dot(left, right, preferred_element_type=jnp.float32, precision=lax.Pr...  30.5 us
    reduce_scatter x3, waiting for transfers between devices, per_device(): lax.psum_scatter(matmul(w_block, spectra), 'px', scatter_dimension=1, til...  28.4 us
    unnamed x3, matrix products  18.9 us
    unnamed x1, blocking collectives  8.37 us
  transfers between devices with their start and end apart: 6, of which 3 were waited for; matrix products, arithmetic and copies ran while one was open for 1% of the time, Pallas kernels for 0%

profile of v1, /device:TPU:0, one launch (start us, length us, event | category | flops | bytes accessed | tf_op | source)
XLA Modules:
  0.0 324.7 jit_solution(12025614497799748229)
XLA Ops:
  7.2 15.3 %all-gather = f32[4,96,48]{1,2,0:T(8,128)S(1)} all-gather(f32[1,96,48]{1,2,0:T(8,128)} %bitcast.92), channel_id=1, replica_groups=mesh['mz'=4,'px'=8] {'mz'}, dimensions={0}, use_global_device_ids=true | all-gather | bytes 92160 | tf_op jit(solution)/shard_map/all_gather | solution.py:14
  22.5 0.1 reshape.37
  22.7 6.1 %fusion.3 = f32[48,3072]{1,0:T(8,128)} fusion(f32[384,48]{0,1:T(8,128)S(1)} %reshape.37, f32[384,3072]{1,0:T(8,128)} %param.3), kind=kOutput, calls=%fused_computation.16 | convolution fusion | flops 679477248 | bytes 5382144 | tf_op jit(solution)/shard_map/dot_general | solution.py:10
  28.8 0.0 reduce-scatter.19.cloned.1.call-start
  28.8 0.2 fusion.4
  29.0 22.5 %psum.42 = f32[48,48]{1,0:T(8,128)S(1)} all-reduce(f32[48,48]{1,0:T(8,128)S(1)} %fusion.4), channel_id=1, replica_groups=mesh['mz'=4,'px'=8] {'px'}, use_global_device_ids=true, to_apply=%region_1.0 | all-reduce | flops 2304 | bytes 18432 | tf_op jit(solution)/shard_map/psum | solution.py:18
  51.5 11.9 %reduce-scatter.13.cloned.1.call-done = f32[48,384]{1,0:T(8,128)} async-done(((f32[48,3072]{1,0:T(8,128)}), f32[48,384]{1,0:T(8,128)}) %reduce-scatter.13.cloned.1.call-update) | async-done | bytes 73744 | tf_op jit(solution)/shard_map/reduce_scatter | solution.py:31
  63.4 1.1 convolution_divide_fusion.2
  64.5 13.0 %all_to_all.15 = f32[8,48,384]{2,1,0:T(8,128)S(1)} all-to-all(f32[8,48,384]{2,1,0:T(8,128)S(1)} %stack.6), channel_id=1, replica_groups=mesh['mz'=4,'px'=8] {'px'}, dimensions={0} | all-to-all | bytes 1179648 | tf_op jit(solution)/shard_map/all_to_all | solution.py:37
  77.5 6.3 %convolution_bitcast_fusion.2 = f32[384,48]{1,0:T(8,128)} fusion(f32[48,3072]{1,0:T(8,128)S(1)} %bitcast.88, f32[384,3072]{1,0:T(8,128)} %param.3), kind=kOutput, calls=%fused_computation.3 | convolution fusion | flops 679477248 | bytes 5382144
  83.9 0.0 reduce-scatter.15.cloned.1.call-start
  83.9 0.6 convolution_bitcast_fusion.5
  84.5 19.2 %psum.43 = f32[48,48]{1,0:T(8,128)S(1)} all-reduce(f32[48,48]{1,0:T(8,128)S(1)} %convolution_bitcast_fusion.5), channel_id=1, replica_groups=mesh['mz'=4,'px'=8] {'mz'}, use_global_device_ids=true, to_apply=%region_3.0 | all-reduce | flops 2304 | bytes 18432 | tf_op jit(solution)/shard_map/psum | solution.py:22
  103.7 0.9 copy.18
  104.6 0.2 convolution_divide_fusion.5
  104.7 13.3 %all-gather.1 = f32[4,96,48]{1,2,0:T(8,128)S(1)} all-gather(f32[1,96,48]{1,2,0:T(8,128)S(1)} %bitcast.91), channel_id=1, replica_groups=mesh['mz'=4,'px'=8] {'mz'}, dimensions={0}, use_global_device_ids=true | all-gather | bytes 92160 | tf_op jit(solution)/shard_map/all_gather | solution.py:14
  118.1 0.1 reshape.39
  118.2 6.1 %fusion.5 = f32[48,3072]{1,0:T(8,128)} fusion(f32[384,48]{0,1:T(8,128)S(1)} %reshape.39, f32[384,3072]{1,0:T(8,128)} %param.3), kind=kOutput, calls=%fused_computation.18 | convolution fusion | flops 679477248 | bytes 5382144 | tf_op jit(solution)/shard_map/dot_general | solution.py:10
  124.3 0.2 fusion.6
  124.5 22.4 %psum.44 = f32[48,48]{1,0:T(8,128)S(1)} all-reduce(f32[48,48]{1,0:T(8,128)S(1)} %fusion.6), channel_id=1, replica_groups=mesh['mz'=4,'px'=8] {'px'}, use_global_device_ids=true, to_apply=%region_5.0 | all-reduce | flops 2304 | bytes 18432 | tf_op jit(solution)/shard_map/psum | solution.py:18
  147.0 8.3 %reduce-scatter.15.cloned.1.call-done = f32[48,384]{1,0:T(8,128)} async-done(((f32[48,3072]{1,0:T(8,128)}), f32[48,384]{1,0:T(8,128)}) %reduce-scatter.15.cloned.1.call-update) | async-done | bytes 73744 | tf_op jit(solution)/shard_map/reduce_scatter | solution.py:31
  155.2 1.1 convolution_divide_fusion.1
  156.4 12.9 %all_to_all.16 = f32[8,48,384]{2,1,0:T(8,128)S(1)} all-to-all(f32[8,48,384]{2,1,0:T(8,128)S(1)} %stack.7), channel_id=1, replica_groups=mesh['mz'=4,'px'=8] {'px'}, dimensions={0} | all-to-all | bytes 1179648 | tf_op jit(solution)/shard_map/all_to_all | solution.py:37
  169.4 6.3 %convolution_bitcast_fusion.1 = f32[384,48]{1,0:T(8,128)} fusion(f32[48,3072]{1,0:T(8,128)S(1)} %bitcast.89, f32[384,3072]{1,0:T(8,128)} %param.3), kind=kOutput, calls=%fused_computation.2 | convolution fusion | flops 679477248 | bytes 5382144
  175.7 0.0 reduce-scatter.17.cloned.1.call-start
  175.8 0.6 convolution_bitcast_fusion.4
  176.4 19.1 %psum.45 = f32[48,48]{1,0:T(8,128)S(1)} all-reduce(f32[48,48]{1,0:T(8,128)S(1)} %convolution_bitcast_fusion.4), channel_id=1, replica_groups=mesh['mz'=4,'px'=8] {'mz'}, use_global_device_ids=true, to_apply=%region_7.0 | all-reduce | flops 2304 | bytes 18432 | tf_op jit(solution)/shard_map/psum | solution.py:22
  195.5 0.9 copy.20
  196.4 0.2 convolution_divide_fusion.4
  196.6 13.3 %all-gather.2 = f32[4,96,48]{1,2,0:T(8,128)S(1)} all-gather(f32[1,96,48]{1,2,0:T(8,128)S(1)} %bitcast.90), channel_id=1, replica_groups=mesh['mz'=4,'px'=8] {'mz'}, dimensions={0}, use_global_device_ids=true | all-gather | bytes 92160 | tf_op jit(solution)/shard_map/all_gather | solution.py:14
  209.9 0.1 reshape.41
  210.0 6.1 %fusion.7 = f32[48,3072]{1,0:T(8,128)} fusion(f32[384,48]{0,1:T(8,128)S(1)} %reshape.41, f32[384,3072]{1,0:T(8,128)} %param.3), kind=kOutput, calls=%fused_computation.20 | convolution fusion | flops 679477248 | bytes 5382144 | tf_op jit(solution)/shard_map/dot_general | solution.py:10
  216.2 0.2 fusion.8
  216.4 22.4 %psum.46 = f32[48,48]{1,0:T(8,128)S(1)} all-reduce(f32[48,48]{1,0:T(8,128)S(1)} %fusion.8), channel_id=1, replica_groups=mesh['mz'=4,'px'=8] {'px'}, use_global_device_ids=true, to_apply=%region_9.0 | all-reduce | flops 2304 | bytes 18432 | tf_op jit(solution)/shard_map/psum | solution.py:18
  238.8 8.2 %reduce-scatter.17.cloned.1.call-done = f32[48,384]{1,0:T(8,128)} async-done(((f32[48,3072]{1,0:T(8,128)}), f32[48,384]{1,0:T(8,128)}) %reduce-scatter.17.cloned.1.call-update) | async-done | bytes 73744 | tf_op jit(solution)/shard_map/reduce_scatter | solution.py:31
  247.0 1.1 convolution_divide_fusion
  248.2 12.9 %all_to_all.17 = f32[8,48,384]{2,1,0:T(8,128)S(1)} all-to-all(f32[8,48,384]{2,1,0:T(8,128)S(1)} %stack.8), channel_id=1, replica_groups=mesh['mz'=4,'px'=8] {'px'}, dimensions={0} | all-to-all | bytes 1179648 | tf_op jit(solution)/shard_map/all_to_all | solution.py:37
  261.2 6.3 %convolution_bitcast_fusion = f32[384,48]{1,0:T(8,128)} fusion(f32[48,3072]{1,0:T(8,128)S(1)} %bitcast.83, f32[384,3072]{1,0:T(8,128)} %param.3), kind=kOutput, calls=%fused_computation.1 | convolution fusion | flops 679477248 | bytes 5382144
  267.5 0.6 dynamic-slice
  268.8 0.6 convolution_bitcast_fusion.3
  269.4 19.0 %psum.47 = f32[48,48]{1,0:T(8,128)S(1)} all-reduce(f32[48,48]{1,0:T(8,128)S(1)} %convolution_bitcast_fusion.3), channel_id=1, replica_groups=mesh['mz'=4,'px'=8] {'mz'}, use_global_device_ids=true, to_apply=%region_11.0 | all-reduce | flops 2304 | bytes 18432 | tf_op jit(solution)/shard_map/psum | solution.py:22
  288.4 0.9 copy.22
  289.3 0.2 convolution_divide_fusion.3
  289.4 13.3 %all-gather.3 = f32[4,96,48]{1,2,0:T(8,128)S(1)} all-gather(f32[1,96,48]{1,2,0:T(8,128)S(1)} %bitcast.93), channel_id=1, replica_groups=mesh['mz'=4,'px'=8] {'mz'}, dimensions={0}, use_global_device_ids=true | all-gather | bytes 92160 | tf_op jit(solution)/shard_map/all_gather | solution.py:14
  302.8 0.1 reshape.43
  302.9 6.0 %multiply_reduce_fusion = f32[384]{0:T(512)S(1)} fusion(f32[384,3072]{1,0:T(8,128)} %param.3, f32[384,48]{0,1:T(8,128)S(1)} %reshape.43, f32[48,3072]{1,0:T(8,128)S(1)} %bitcast.84), kind=kOutput, calls=%fused_computation | convolution fusion | flops 683015808 | bytes 5383680 | tf_op jit(solution)/shard_map/dot_general | solution.py:10
  308.9 8.4 %all-reduce = f32[384]{0:T(512)S(1)} all-reduce(f32[384]{0:T(512)S(1)} %multiply_reduce_fusion), channel_id=8, replica_groups=mesh['mz'=4,'px'=8] {'mz'}, use_global_device_ids=true, to_apply=%region_13.0.clone | all-reduce | flops 384 | bytes 3072
  317.3 0.6 dynamic-slice.1
  (32 shorter events, 0.7 us)
Async XLA Ops:
  7.2 56.2 %copy-start.3 = (f32[48,384]{1,0:T(8,128)S(1)}, f32[48,384]{1,0:T(8,128)}, u32[]{:S(2)}) copy-start(f32[48,384]{1,0:T(8,128)} %param.5) | copy-start | bytes 221188
  7.2 56.2 %reduce-scatter.13.cloned.1.call-start = ((), (), s32[]{:S(2)}) async-start(), calls=%async_computation.9 | async-start | bytes 663552 | tf_op jit(solution)/shard_map/reduce_scatter | solution.py:31
  28.8 74.9 %reduce-scatter.19.cloned.1.call-start = ((), (), s32[]{:S(2)}) async-start(), calls=%async_computation.12 | async-start | bytes 245760
  64.5 40.1 %copy-start = (f32[48,96]{1,0:T(8,128)S(1)}, f32[48,96]{1,0:T(8,128)}, u32[]{:S(2)}) copy-start(f32[48,96]{1,0:T(8,128)} %param.4) | copy-start | bytes 55300
  83.9 71.4 %reduce-scatter.15.cloned.1.call-start = ((), (), s32[]{:S(2)}) async-start(), calls=%async_computation.10 | async-start | bytes 663552 | tf_op jit(solution)/shard_map/reduce_scatter | solution.py:31
  124.3 71.2 %reduce-scatter.21.cloned.1.call-start = ((), (), s32[]{:S(2)}) async-start(), calls=%async_computation.13 | async-start | bytes 245760
  175.7 71.3 %reduce-scatter.17.cloned.1.call-start = ((), (), s32[]{:S(2)}) async-start(), calls=%async_computation.11 | async-start | bytes 663552 | tf_op jit(solution)/shard_map/reduce_scatter | solution.py:31
  216.1 51.4 %copy-start.4 = (u32[32]{0:T(128)S(1)}, u32[32]{0:T(128)}, u32[]{:S(2)}) copy-start(u32[32]{0:T(128)} %constant.4) | copy-start | bytes 388
  216.1 72.3 %reduce-scatter.23.cloned.1.call-start = ((), (), s32[]{:S(2)}) async-start(), calls=%async_computation.14 | async-start | bytes 245760
  248.1 41.1 %copy-start.2 = (f32[48,384]{1,0:T(8,128)}, f32[48,384]{1,0:T(8,128)S(1)}, u32[]{:S(2)}) copy-start(f32[48,384]{1,0:T(8,128)S(1)} %convolution_divide_fusion) | copy-start | bytes 221188
  289.4 28.4 %copy-start.1 = (f32[48,96]{1,0:T(8,128)}, f32[48,96]{1,0:T(8,128)S(1)}, u32[]{:S(2)}) copy-start(f32[48,96]{1,0:T(8,128)S(1)} %convolution_divide_fusion.3) | copy-start | bytes 55300
Sparse Core Ops, SparseCore 0:
  28.9 34.4 reduce-scatter.12
  84.0 18.9 reduce-scatter.18
  124.4 30.7 reduce-scatter.14
  175.8 18.9 reduce-scatter.20
  216.2 30.7 reduce-scatter.16
  267.6 18.8 reduce-scatter.22
